TPU v7x, 32 devices: a whole 2x2x4 slice. The times are simulated.
32 devices in a mesh: dp: 8 (over y, x, core), fsdp: 4 (over z).
Axes of the slice: x: 2, y: 2, z: 4, core: 2. Of those that a mesh axis runs over, the one named last changes fastest.
Arguments:
- tokens: bfloat16 [16384, 1024], P(('dp', 'fsdp')), may hold values from -20 to 20
- w_qkv: bfloat16 [1024, 3072], P('fsdp'), may hold values from -0.1875 to 0.1875
- w_out: bfloat16 [1024, 1024], P('fsdp'), may hold values from -0.1875 to 0.1875
- doc_blocks: int32 [32, 4], P(('dp', 'fsdp')), may hold values from 0 to 1, never falling along the last dimension, each value on 1 to 3 neighbouring positions
- cotangent: bfloat16 [16384, 1024], P(('dp', 'fsdp')), may hold values from -6 to 6
Outputs:
- output: bfloat16 [16384, 1024], P(('dp', 'fsdp'))
- grad_tokens: bfloat16 [16384, 1024], P(('dp', 'fsdp'))
- grad_w_qkv: float32 [1024, 3072], P('fsdp')
- grad_w_out: float32 [1024, 1024], P('fsdp')
Inputs may be any that keep to these rules, and one draw needn't show every extreme that they name: `doc_blocks`: ids never fall along a sequence; each of the 2 documents of a sequence covers 1 to 3 blocks.
All inputs are finite; a program needn't handle non-finite values.
Results may differ from a plain program's by a relative error of at most 0.012.
Values may be sent and summed in bfloat16 or wider, within the bound.
A program may use at most 128 MiB of HBM per device.

v0:
```python
import math
import jax
import jax.numpy as jnp
from jax import lax
from jax.sharding import PartitionSpec as P

H = 8
NEG_FILL = -1e30
CONTRACT_ROWS = (((0,), (0,)), ((), ()))
CONTRACT_COLS = (((1,), (1,)), ((), ()))


def row_mask(doc_ids, row_count):
    block_len = row_count // doc_ids.shape[0]
    doc_rows = jnp.repeat(doc_ids, block_len, total_repeat_length=row_count)
    position = jnp.arange(row_count, dtype=jnp.int32)
    causal = position[None, :] <= position[:, None]
    return causal & (doc_rows[None, :] == doc_rows[:, None])


def split_heads(matrix, head_count):
    return matrix.reshape(matrix.shape[0], head_count, matrix.shape[1] // head_count)


def attend_forward(query_rows, key_rows, value_rows, allowed, head_count):
    row_count = query_rows.shape[0]
    query_heads = split_heads(query_rows, head_count)
    key_heads = split_heads(key_rows, head_count)
    value_heads = split_heads(value_rows, head_count)
    score_scale = query_heads.shape[2] ** (-0.5)
    scores = (
        jnp.einsum("qhd,khd->hqk", query_heads, key_heads, preferred_element_type=jnp.float32)
        * score_scale
    )
    scores = jnp.where(allowed[None], scores, NEG_FILL)
    highest = jnp.max(scores, axis=-1, keepdims=True)
    expvals = jnp.exp(scores - highest)
    attn_probs = expvals / jnp.sum(expvals, axis=-1, keepdims=True)
    probs_half = attn_probs.astype(jnp.bfloat16)
    mixed = jnp.einsum("hqk,khd->qhd", probs_half, value_heads, preferred_element_type=jnp.float32)
    return (mixed.astype(jnp.bfloat16).reshape(row_count, -1), attn_probs, probs_half)


def attend_backward(
    query_rows, key_rows, value_rows, attn_probs, probs_half, grad_mixed, head_count
):
    row_count = query_rows.shape[0]
    query_heads = split_heads(query_rows, head_count)
    key_heads = split_heads(key_rows, head_count)
    value_heads = split_heads(value_rows, head_count)
    grad_heads = split_heads(grad_mixed, head_count)
    score_scale = query_heads.shape[2] ** (-0.5)
    grad_probs = jnp.einsum(
        "qhd,khd->hqk", grad_heads, value_heads, preferred_element_type=jnp.float32
    )
    grad_values = jnp.einsum(
        "hqk,qhd->khd", probs_half, grad_heads, preferred_element_type=jnp.float32
    )
    inner = jnp.sum(attn_probs * grad_probs, axis=-1, keepdims=True)
    grad_scores = (attn_probs * (grad_probs - inner)).astype(jnp.bfloat16)
    grad_queries = (
        jnp.einsum("hqk,khd->qhd", grad_scores, key_heads, preferred_element_type=jnp.float32)
        * score_scale
    )
    grad_keys = (
        jnp.einsum("hqk,qhd->khd", grad_scores, query_heads, preferred_element_type=jnp.float32)
        * score_scale
    )
    pieces_list = [grad_queries, grad_keys, grad_values]
    return jnp.concatenate(
        [p.astype(jnp.bfloat16).reshape(row_count, -1) for p in pieces_list], axis=1
    )


def body(tokens, w_qkv, w_out, doc_blocks, cotangent):
    row_count = tokens.shape[0]
    head_width = w_out.shape[1]
    head_count = H
    all_devices = lax.axis_size("dp") * lax.axis_size("fsdp")
    allowed = row_mask(doc_blocks[0], row_count)
    columns = tokens
    qkv = jnp.dot(
        columns,
        lax.all_gather(w_qkv, "fsdp", axis=0, tiled=True),
        preferred_element_type=jnp.float32,
    ).astype(jnp.bfloat16)
    query_rows = qkv[:, :head_width]
    key_rows = qkv[:, head_width : 2 * head_width]
    value_rows = qkv[:, 2 * head_width :]
    mixed, attn_probs, probs_half = attend_forward(
        query_rows, key_rows, value_rows, allowed, head_count
    )
    output = lax.dot_general(
        mixed,
        lax.all_gather(w_out, "fsdp", axis=0, tiled=True),
        CONTRACT_COLS,
        preferred_element_type=jnp.float32,
    )
    columns = cotangent
    grad_mixed = jnp.dot(
        columns,
        lax.all_gather(w_out, "fsdp", axis=0, tiled=True),
        preferred_element_type=jnp.float32,
    ).astype(jnp.bfloat16)
    output = output.astype(jnp.bfloat16)
    grad_qkv = attend_backward(
        query_rows, key_rows, value_rows, attn_probs, probs_half, grad_mixed, head_count
    )
    grad_tokens = lax.dot_general(
        grad_qkv,
        lax.all_gather(w_qkv, "fsdp", axis=0, tiled=True),
        CONTRACT_COLS,
        preferred_element_type=jnp.float32,
    )
    grad_tokens = grad_tokens.astype(jnp.bfloat16)
    first_term = lax.dot_general(
        tokens, grad_qkv, CONTRACT_ROWS, preferred_element_type=jnp.float32
    )
    second_term = lax.dot_general(
        cotangent, mixed, CONTRACT_ROWS, preferred_element_type=jnp.float32
    )
    partial_grad = lax.psum_scatter(
        jnp.concatenate([first_term, second_term], axis=1), "fsdp", scatter_dimension=0, tiled=True
    )
    summed = lax.psum(partial_grad, "dp")
    norm_factor = 1.0 / math.sqrt(row_count * all_devices)
    grad_w_qkv = summed[:, : 3 * head_width] * norm_factor
    grad_w_out = summed[:, 3 * head_width :] * norm_factor
    return (output, grad_tokens, grad_w_qkv, grad_w_out)


def solution(mesh):
    placed = (
        P(("dp", "fsdp"), None),
        P("fsdp", None),
        P("fsdp", None),
        P(("dp", "fsdp"), None),
        P(("dp", "fsdp"), None),
    )
    return jax.shard_map(
        body,
        mesh=mesh,
        in_specs=placed,
        out_specs=(
            P(("dp", "fsdp"), None),
            P(("dp", "fsdp"), None),
            P("fsdp", None),
            P("fsdp", None),
        ),
        check_vma=False,
    )
```

profile of v0, /device:TPU:0, one launch (start us, length us, event | category | flops | bytes accessed | tf_op | source)
XLA Modules:
  0.0 596.9 jit_solution(12965069515736910643)
XLA Ops:
  8.7 1.4 fusion.30
  10.1 2.6 compare_select_fusion.1
  13.0 45.0 %all-gather.5.cloned.1.call-done = bf16[1024,1024]{1,0:T(8,128)(2,1)} async-done(((bf16[256,1024]{1,0:T(8,128)(2,1)}), bf16[1024,1024]{1,0:T(8,128)(2,1)}) %all-gather.5.cloned.1.call-update) | async-done | bytes 2097168 | tf_op jit(solution)/shard_map/all_gather | solution.py:95
  58.0 3.2 convolution_convert_fusion.1
  61.1 1.3 copy.29
  62.5 111.2 %all-gather.3.cloned.1.call-done = bf16[1024,3072]{1,0:T(8,128)(2,1)} async-done(((bf16[256,3072]{1,0:T(8,128)(2,1)}), bf16[1024,3072]{1,0:T(8,128)(2,1)}) %all-gather.3.cloned.1.call-update) | async-done | bytes 6291472 | tf_op jit(solution)/shard_map/all_gather | solution.py:84
  173.7 6.4 %convolution_convert_fusion = bf16[512,3072]{1,0:T(8,128)(2,1)S(1)} fusion(bf16[512,1024]{1,0:T(8,128)(2,1)S(1)} %copy-done, bf16[1024,3072]{1,0:T(8,128)(2,1)} %all-gather.3.cloned.1.call-done), kind=kOutput, calls=%fused_computation.8 | convolution fusion | flops 3222798336 | bytes 10485760 | tf_op jit(solution)/shard_map/dot_general | solution.py:82
  180.1 1.8 fusion.29
  182.5 1.5 copy.28
  184.0 5.4 fusion.31
  189.4 4.7 fusion.9
  194.2 1.7 copy-done.1
  196.1 1.5 fusion.12
  197.7 1.5 multiply_reduce_fusion
  199.2 2.7 multiply_convert_fusion
  201.9 1.5 multiply_convert_fusion.1
  206.3 3.5 convolution_bitcast_fusion
  209.8 7.2 %pad_maximum_fusion = f32[1024,4096]{0,1:T(8,128)} fusion(f32[1024,1024]{0,1:T(8,128)S(1)} %convolution_bitcast_fusion.1, f32[1024,3072]{0,1:T(8,128)S(1)} %convolution_bitcast_fusion), kind=kLoop, calls=%fused_computation.1 | loop fusion | flops 4194304 | bytes 33554432 | tf_op jit(solution)/shard_map/concatenate | solution.py:123
  217.2 278.7 %reduce-scatter.2.cloned.1.call-done = f32[256,4096]{0,1:T(8,128)} async-done(((f32[1024,4096]{0,1:T(8,128)}), f32[256,4096]{0,1:T(8,128)}) %reduce-scatter.2.cloned.1.call-update) | async-done | bytes 4194320 | tf_op jit(solution)/shard_map/reduce_scatter | solution.py:122
  495.9 4.0 convolution_convert_fusion.2
  499.9 7.2 %convolution_convert_fusion.3 = bf16[512,1024]{1,0:T(8,128)(2,1)} fusion(bf16[1024,3072]{1,0:T(8,128)(2,1)} %all-gather.3.cloned.1.call-done, bf16[512,1024]{0,1:T(8,128)(2,1)S(1)} %bitcast.77, bf16[512,1024]{0,1:T(8,128)(2,1)S(1)} %bitcast.70, bf16[512,1024]{0,1:T(8,128)(2,1)S(1)} %bitcast.72), kind=kOutput, calls=%fused_computation.26 | convolution fusion | flops 3231186944 | bytes 10485760 | tf_op jit(solution)/shard_map/dot_general | solution.py:109
  507.1 73.3 %all-reduce.2.cloned.1.call-done = f32[256,4096]{0,1:T(8,128)} async-done(((f32[256,4096]{0,1:T(8,128)}), f32[256,4096]{0,1:T(8,128)}) %all-reduce.2.cloned.1.call-update) | async-done | bytes 4194320 | tf_op jit(solution)/shard_map/psum | solution.py:125
  580.4 3.8 slice_multiply_fusion
  584.2 3.5 copy.21
  (38 shorter events, 8.1 us)
Async XLA Ops:
  7.2 166.5 %copy-start = (bf16[512,1024]{1,0:T(8,128)(2,1)S(1)}, bf16[512,1024]{1,0:T(8,128)(2,1)}, u32[]{:S(2)}) copy-start(bf16[512,1024]{1,0:T(8,128)(2,1)} %param.7) | copy-start | bytes 3145732
  7.2 50.8 %all-gather.5.cloned.1.call-start = ((), (), s32[]{:S(2)}) async-start(), calls=%async_computation.2 | async-start | bytes 2621440 | tf_op jit(solution)/shard_map/all_gather | solution.py:95
  7.9 165.8 %all-gather.3.cloned.1.call-start = ((), (), s32[]{:S(2)}) async-start(), calls=%async_computation.1 | async-start | bytes 7864320 | tf_op jit(solution)/shard_map/all_gather | solution.py:84
  8.7 487.2 %reduce-scatter.2.cloned.1.call-start = ((), (), s32[]{:S(2)}) async-start(), calls=%async_computation.3 | async-start | bytes 20971520 | tf_op jit(solution)/shard_map/reduce_scatter | solution.py:122
  189.4 6.5 %copy-start.1 = (f32[8,512,512]{1,2,0:T(8,128)S(1)}, f32[8,512,512]{1,2,0:T(8,128)}, u32[]{:S(2)}) copy-start(f32[8,512,512]{1,2,0:T(8,128)} %get-tuple-element.28) | copy-start | bytes 25165828
  189.4 6.7 %copy-start.2 = (bf16[512,1024]{0,1:T(8,128)(2,1)S(1)}, bf16[512,1024]{0,1:T(8,128)(2,1)}, u32[]{:S(2)}) copy-start(bf16[512,1024]{0,1:T(8,128)(2,1)} %copy.29) | copy-start | bytes 3145732
  194.1 10.0 %copy-start.9 = (bf16[8,128,512]{2,1,0:T(8,128)(2,1)}, bf16[8,128,512]{2,1,0:T(8,128)(2,1)S(1)}, u32[]{:S(2)}) copy-start(bf16[8,128,512]{2,1,0:T(8,128)(2,1)S(1)} %fusion.9) | copy-start | bytes 3145732
  196.1 1.5 copy-start.5
  197.6 8.6 %copy-start.7 = (bf16[8,128,512]{2,1,0:T(8,128)(2,1)}, bf16[8,128,512]{2,1,0:T(8,128)(2,1)S(1)}, u32[]{:S(2)}) copy-start(bf16[8,128,512]{2,1,0:T(8,128)(2,1)S(1)} %fusion.12) | copy-start | bytes 3145732
  203.4 2.9 copy-start.3
  203.4 1.6 copy-start.6
  217.1 278.8 %copy-start.10 = (bf16[8,128,512]{2,1,0:T(8,128)(2,1)S(1)}, bf16[8,128,512]{2,1,0:T(8,128)(2,1)}, u32[]{:S(2)}) copy-start(bf16[8,128,512]{2,1,0:T(8,128)(2,1)} %copy-done.9) | copy-start | bytes 3145732
  217.1 363.3 %all-reduce.2.cloned.1.call-start = ((), (), s32[]{:S(2)}) async-start(), calls=%async_computation.4 | async-start | bytes 8388608 | tf_op jit(solution)/shard_map/psum | solution.py:125
  495.9 4.0 copy-start.4
  495.9 4.0 copy-start.8
Sparse Core Ops, SparseCore 0:
  9.6 48.3 all-gather.4
  59.5 114.1 all-gather.2
  217.2 278.5 reduce-scatter.1
  499.0 81.4 all-reduce.1
where the time goes:
time: 597 us
  waiting for transfers between devices  510 us (85%)
  matrix products  41 us (7%)
  other arithmetic  17.8 us (3%)
  local copies, waits for them, and re-layouts  14.3 us (2%)
  between operations  14 us (2%)
    reduce_scatter x1, waiting for transfers between devices, body(): lax.psum_scatter(jnp.concatenate([first_term, second_term], axis=1), 'fsd...  279 us
    all_gather x1, waiting for transfers between devices, body(): lax.all_gather(w_qkv, 'fsdp', axis=0, tiled=True)  111 us
    psum x1, waiting for transfers between devices, body(): summed = lax.psum(partial_grad, 'dp')  73.3 us
    all_gather x1, waiting for transfers between devices, body(): lax.all_gather(w_out, 'fsdp', axis=0, tiled=True)  45 us
  transfers between devices with their start and end apart: 4, of which 4 were waited for; matrix products, arithmetic and copies ran while one was open for 3% of the time, Pallas kernels for 0%

commit v1 on v0

--- a/solution.py
+++ b/solution.py
@@ -122,7 +122,7 @@
     partial_grad = lax.psum_scatter(
         jnp.concatenate([first_term, second_term], axis=1), "fsdp", scatter_dimension=0, tiled=True
     )
-    summed = lax.psum(partial_grad, "dp")
+    summed = jnp.sum(lax.all_gather(partial_grad, "dp"), axis=0)
     norm_factor = 1.0 / math.sqrt(row_count * all_devices)
     grad_w_qkv = summed[:, : 3 * head_width] * norm_factor
     grad_w_out = summed[:, 3 * head_width :] * norm_factor

time: 597 us -> 723 us (1.21)
  waiting for transfers between devices: 510 us -> 595 us
  other arithmetic: 17.8 us -> 39.5 us
  local copies, waits for them, and re-layouts: 14.3 us -> 32.6 us
    all_gather x0 -> x1, waiting for transfers between devices: none -> 158 us  [body(): summed = jnp.sum(lax.all_gather(partial_grad, 'dp'), axis=0)]
    psum x1 -> x0, waiting for transfers between devices: 73.3 us -> none  [body(): summed = lax.psum(partial_grad, 'dp')]
    reduce_sum x0 -> x1, other arithmetic: none -> 21.7 us  [body(): summed = jnp.sum(lax.all_gather(partial_grad, 'dp'), axis=0)]
    unnamed x24 -> x25, local copies, waits for them, and re-layouts: 7.69 us -> 26 us
where the time goes in v1:
time: 723 us; the launch traced here: 722 us
  waiting for transfers between devices  595 us (82%)
  matrix products  41.3 us (6%)
  other arithmetic  39.5 us (5%)
  local copies, waits for them, and re-layouts  32.6 us (5%)
  between operations  14 us (2%)
    reduce_scatter x1, waiting for transfers between devices, body(): lax.psum_scatter(jnp.concatenate([first_term, second_term], axis=1), 'fsd...  279 us
    all_gather x1, waiting for transfers between devices, body(): summed = jnp.sum(lax.all_gather(partial_grad, 'dp'), axis=0)  158 us
    all_gather x1, waiting for transfers between devices, body(): lax.all_gather(w_qkv, 'fsdp', axis=0, tiled=True)  111 us
    all_gather x1, waiting for transfers between devices, body(): lax.all_gather(w_out, 'fsdp', axis=0, tiled=True)  45 us
    unnamed x25, local copies, waits for them, and re-layouts  26 us
    reduce_sum x1, other arithmetic, body(): summed = jnp.sum(lax.all_gather(partial_grad, 'dp'), axis=0)  21.7 us
  transfers between devices with their start and end apart: 4, of which 4 were waited for; matrix products, arithmetic and copies ran while one was open for 3% of the time, Pallas kernels for 0%

profile of v1, /device:TPU:0, one launch (start us, length us, event | category | flops | bytes accessed | tf_op | source)
XLA Modules:
  0.0 722.1 jit_solution(15414473233562654689)
XLA Ops:
  8.7 1.4 fusion.30
  10.1 2.6 compare_select_fusion.1
  13.0 45.0 %all-gather.7.cloned.1.call-done = bf16[1024,1024]{1,0:T(8,128)(2,1)} async-done(((bf16[256,1024]{1,0:T(8,128)(2,1)}), bf16[1024,1024]{1,0:T(8,128)(2,1)}) %all-gather.7.cloned.1.call-update) | async-done | bytes 2097168 | tf_op jit(solution)/shard_map/all_gather | solution.py:95
  58.0 3.2 convolution_convert_fusion.1
  62.5 111.2 %all-gather.5.cloned.1.call-done = bf16[1024,3072]{1,0:T(8,128)(2,1)} async-done(((bf16[256,3072]{1,0:T(8,128)(2,1)}), bf16[1024,3072]{1,0:T(8,128)(2,1)}) %all-gather.5.cloned.1.call-update) | async-done | bytes 6291472 | tf_op jit(solution)/shard_map/all_gather | solution.py:84
  173.7 6.4 convolution_convert_fusion
  180.1 1.8 fusion.29
  182.4 1.5 copy.39
  183.9 5.4 fusion.31
  189.4 5.3 fusion.12
  196.9 1.5 multiply_reduce_fusion
  198.4 2.7 multiply_convert_fusion
  201.1 1.5 multiply_convert_fusion.1
  204.6 3.6 convolution_bitcast_fusion
  208.2 7.1 pad_maximum_fusion
  215.4 278.8 %reduce-scatter.2.cloned.1.call-done = f32[256,4096]{0,1:T(8,128)} async-done(((f32[1024,4096]{0,1:T(8,128)}), f32[256,4096]{0,1:T(8,128)}) %reduce-scatter.2.cloned.1.call-update) | async-done | bytes 4194320 | tf_op jit(solution)/shard_map/reduce_scatter | solution.py:122
  494.2 4.3 convolution_convert_fusion.2
  498.5 7.2 convolution_convert_fusion.3
  505.7 158.1 %all-gather.9.cloned.1.call-done = f32[2048,4096]{0,1:T(8,128)} async-done(((f32[256,4096]{0,1:T(8,128)}), f32[2048,4096]{0,1:T(8,128)}) %all-gather.9.cloned.1.call-update) | async-done | bytes 33554448 | tf_op jit(solution)/shard_map/all_gather | solution.py:125
  663.9 19.9 %copy.43 = f32[512,8,8,256]{3,2,1,0:T(8,128)S(1)} copy(f32[512,8,8,256]{3,1,2,0:T(8,128)} %bitcast.68) | data formatting | bytes 67108864
  683.8 21.7 %bitcast_reduce_fusion = f32[256,4096]{0,1:T(8,128)} fusion(f32[512,8,8,256]{3,2,1,0:T(8,128)S(1)} %copy.43), kind=kLoop, calls=%fused_computation.1 | loop fusion | flops 7340032 | bytes 37748736 | tf_op jit(solution)/shard_map/reduce_sum | solution.py:125
  705.5 1.4 slice_multiply_fusion.1
  706.9 3.8 slice_multiply_fusion
  710.7 3.5 copy.33
  (40 shorter events, 9.2 us)
Async XLA Ops:
  7.2 166.5 %copy-start = (bf16[512,1024]{1,0:T(8,128)(2,1)S(1)}, bf16[512,1024]{1,0:T(8,128)(2,1)}, u32[]{:S(2)}) copy-start(bf16[512,1024]{1,0:T(8,128)(2,1)} %param.7) | copy-start | bytes 3145732
  7.2 50.8 %all-gather.7.cloned.1.call-start = ((), (), s32[]{:S(2)}) async-start(), calls=%async_computation.2 | async-start | bytes 2621440 | tf_op jit(solution)/shard_map/all_gather | solution.py:95
  7.9 165.8 %all-gather.5.cloned.1.call-start = ((), (), s32[]{:S(2)}) async-start(), calls=%async_computation.1 | async-start | bytes 7864320 | tf_op jit(solution)/shard_map/all_gather | solution.py:84
  8.7 485.5 %reduce-scatter.2.cloned.1.call-start = ((), (), s32[]{:S(2)}) async-start(), calls=%async_computation.3 | async-start | bytes 20971520 | tf_op jit(solution)/shard_map/reduce_scatter | solution.py:122
  189.4 6.1 copy-start.2
  189.4 6.3 copy-start.6
  194.7 9.9 %copy-start.8 = (bf16[8,128,512]{2,1,0:T(8,128)(2,1)}, bf16[8,128,512]{2,1,0:T(8,128)(2,1)S(1)}, u32[]{:S(2)}) copy-start(bf16[8,128,512]{2,1,0:T(8,128)(2,1)S(1)} %fusion.12) | copy-start | bytes 3145732
  195.7 1.2 copy-start.3
  196.9 6.4 copy-start.10
  201.1 2.3 copy-start.7
  202.6 2.0 copy-start.4
  215.3 448.5 %all-gather.9.cloned.1.call-start = ((), (), s32[]{:S(2)}) async-start(), calls=%async_computation.4 | async-start | bytes 37748736 | tf_op jit(solution)/shard_map/all_gather | solution.py:125
  494.2 4.4 copy-start.5
  494.2 4.4 copy-start.9
  705.5 10.0 %copy-start.1 = (bf16[512,1024]{1,0:T(8,128)(2,1)S(1)}, bf16[512,1024]{1,0:T(8,128)(2,1)}, u32[]{:S(2)}) copy-start(bf16[512,1024]{1,0:T(8,128)(2,1)} %param.7) | copy-start | bytes 3145732
Sparse Core Ops, SparseCore 0:
  9.6 48.3 all-gather.6
  59.5 114.1 all-gather.4
  215.5 278.6 reduce-scatter.1
  495.9 167.9 all-gather.8
